TPU v7x, 1024 devices: a whole 4x8x16 slice. The times are simulated.
1024 devices in a mesh: lat: 16 (over x, y_lo, core), lev: 64 (over z, y_hi).
Axes of the slice: x: 4, y: 8 (y_hi: 4, y_lo: 2; y = y_hi * 2 + y_lo), z: 16, core: 2. Of those that a mesh axis runs over, the one named last changes fastest.
Arguments:
- fields: bfloat16 [6, 128, 128, 1152], P(None, 'lev', 'lat'), may hold values from -6 to 6
- courant: bfloat16 [128, 128, 1152], P('lev', 'lat'), may hold values from -0.8984375 to 0.8984375
- filter_matrix: bfloat16 [1152, 1152], replicated, may hold values from -0.1875 to 0.1875
- polar_mask: int32 [128], P('lat'), may hold values from 0 to 1, as said below
- band_start: int32 [128], replicated, may hold values from 0 to 124, as said below
- remap_weights: float32 [128, 128, 4], P('lat'), may hold values from 0.05 to 0.5
Outputs:
- remapped: bfloat16 [6, 128, 128, 1152], P(None, 'lev', 'lat')
Inputs may be any that keep to these rules, and one draw needn't show every extreme that they name: `polar_mask`: 1 on a run of 16 to 32 latitudes at each pole, 0 elsewhere. band_start[0] is 0 and band_start[127] is 124.
All inputs are finite; a program needn't handle non-finite values.
Results may differ from a plain program's by a relative error of at most 0.0052.
Values may be sent and summed in bfloat16 or wider, within the bound.
A program may use at most 32 MiB of HBM per device.

v0:
```python
import jax
import jax.numpy as jnp
from jax import lax
from jax.sharding import Mesh
from jax.sharding import PartitionSpec as P

LEV = ("lev_0", "lev_1")


def padded_2(block, sides, width):
    for axis, dim in sides:
        count = lax.axis_size(axis)
        forward = [(i, i + 1) for i in range(count - 1)]
        backward = [(target, source) for source, target in forward]
        low = lax.ppermute(
            lax.slice_in_dim(block, block.shape[dim] - width, None, axis=dim), axis, forward
        )
        high = lax.ppermute(lax.slice_in_dim(block, 0, width, axis=dim), axis, backward)
        block = jnp.concatenate([low, block, high], axis=dim)
    return block


def split_up(value, dim, devices):
    before, after = (value.shape[:dim], value.shape[dim + 1 :])
    return jnp.moveaxis(value.reshape(*before, devices, -1, *after), dim, 0)


def in_order(pieces, dim):
    pieces = jnp.moveaxis(pieces, 0, dim)
    dims = pieces.shape
    return pieces.reshape(*dims[:dim], dims[dim] * dims[dim + 1], *dims[dim + 2 :])


def exchange_in_order(pieces, axes, sequence):
    dims = [lax.axis_size(a) for a in axes]
    pieces = pieces.reshape(*dims, *pieces.shape[1:])
    for k in sequence:
        pieces = lax.all_to_all(pieces, axes[k], split_axis=k, concat_axis=k, tiled=True)
    return pieces.reshape(-1, *pieces.shape[len(axes) :])


def one_axis_at_a_time(value, axes, sequence, split_dim, concat_dim):
    pieces = split_up(value, split_dim, lax.axis_size(axes))
    return in_order(exchange_in_order(pieces, axes, sequence), concat_dim)


def on_device(fields, courant, filter_matrix, polar_mask, band_start, remap_weights):
    field_count = fields.shape[0]
    level_rows = fields.shape[1]
    lat_rows = fields.shape[2]
    lon_total = fields.shape[3]
    band_width = remap_weights.shape[2]
    level_total = band_start.shape[0]
    lat_total = lat_rows * lax.axis_size("lat")
    first_row = lax.axis_index("lat") * lat_rows
    stacked = jnp.concatenate([fields, courant[None]], axis=0)
    extended = padded_2(stacked, (("lat", 2),), 2)
    padded = extended[:field_count].astype(jnp.float32)
    speed_pad = extended[field_count].astype(jnp.float32)
    face_index = first_row + jnp.arange(lat_rows + 1, dtype=jnp.int32) - 1
    face_live = ((face_index >= 0) & (face_index <= lat_total - 2)).astype(jnp.float32)[
        None, :, None
    ]
    face_speed = 0.5 * (speed_pad[:, 1 : lat_rows + 2] + speed_pad[:, 2 : lat_rows + 3]) * face_live
    face_flux = (
        face_speed[None]
        * (
            7.0 * (padded[:, :, 1 : lat_rows + 2] + padded[:, :, 2 : lat_rows + 3])
            - (padded[:, :, 0 : lat_rows + 1] + padded[:, :, 3 : lat_rows + 4])
        )
        / 12.0
    )
    moved_field = padded[:, :, 2 : lat_rows + 2] - (face_flux[:, :, 1:] - face_flux[:, :, :-1])
    moved_low = moved_field.astype(jnp.bfloat16)
    correction = jnp.dot(
        moved_low.reshape(-1, lon_total), filter_matrix, preferred_element_type=jnp.float32
    ).reshape(moved_field.shape)
    polar_rows = (polar_mask == 1)[None, None, :, None]
    filtered = (moved_field + jnp.where(polar_rows, correction, 0.0)).astype(jnp.bfloat16)
    flat_cells = lat_rows * lon_total
    flat_filtered = filtered.reshape(field_count, level_rows, flat_cells)
    piece_cells = flat_cells // lax.axis_size(LEV)
    cell_index = lax.axis_index(LEV) * piece_cells + jnp.arange(piece_cells, dtype=jnp.int32)
    cell_lat = cell_index // lon_total
    lat_onehot = (jnp.arange(lat_rows, dtype=jnp.int32)[:, None] == cell_lat[None, :]).astype(
        jnp.float32
    )
    band_weights = jnp.transpose(remap_weights, (2, 1, 0))
    cell_weights = jnp.einsum(
        "btl,lp->btp", band_weights, lat_onehot, precision=lax.Precision.HIGHEST
    )
    source_index = jnp.arange(level_total, dtype=jnp.int32)[None, None, :]
    band_offset = jnp.arange(band_width, dtype=jnp.int32)[:, None, None]
    selection = (source_index == band_start[None, :, None] + band_offset).astype(jnp.bfloat16)
    columns = one_axis_at_a_time(flat_filtered, LEV, (0, 1), 2, 1)
    total = jnp.zeros(columns.shape, jnp.float32)
    for offset in range(band_width):
        source = jnp.einsum(
            "ts,fsp->ftp", selection[offset], columns, preferred_element_type=jnp.float32
        )
        total = total + cell_weights[offset][None] * source
    flat_out = lax.all_to_all(
        total.astype(jnp.bfloat16), LEV, split_axis=1, concat_axis=2, tiled=True
    )
    return flat_out.reshape(field_count, level_rows, lat_rows, lon_total)


def solution(mesh):
    finer = Mesh(mesh.devices.reshape(mesh.shape["lat"], 16, 4), ("lat", "lev_0", "lev_1"))
    placed = (
        P(None, LEV, "lat", None),
        P(LEV, "lat", None),
        P(),
        P("lat"),
        P(),
        P("lat", None, None),
    )
    return jax.shard_map(
        on_device, mesh=finer, in_specs=placed, out_specs=P(None, LEV, "lat", None), check_vma=False
    )
```

profile of v0, /device:TPU:2, one launch (start us, length us, event | category | flops | bytes accessed | tf_op | source)
XLA Modules:
  0.0 119.6 jit_solution(3384545851195381022)
XLA Ops:
  0.0 0.0 copy-start
  0.0 0.0 copy-start.2
  0.0 0.0 copy-start.1
  0.0 1.3 %pad_maximum_fusion.2 = (bf16[7,2,2,1152]{3,2,1,0:T(2,128)(2,1)S(1)}, bf16[7,2,2,1152]{3,2,1,0:T(2,128)(2,1)S(1)}) fusion(bf16[1,2,8,1152]{3,2,1,0:T(8,128)(2,1)} %bitcast.96, bf16[6,2,8,1152]{3,2,1,0:T(8,128)(2,1)} %param.6), kind=kLoop, calls=%fused_computation.44 | loop fusion | flops 258048 | bytes 387072 | tf_op jit(solution)/shard_map/slice | solution.py:16
  1.3 1.9 %collective-permute-start = (bf16[7,2,2,1152]{3,2,1,0:T(2,128)(2,1)S(1)}, bf16[7,2,2,1152]{3,2,1,0:T(2,128)(2,1)S(1)}, u32[]{:S(2)}, u32[]{:S(2)}) collective-permute-start(bf16[7,2,2,1152]{3,2,1,0:T(2,128)(2,1)S(1)} %get-tuple-element.9), channel_id=1, source_target_pairs={{0,64},{64,128},{128,192},{192,256},{256,320},{320,384},{384,448},... | collective-permute-start | bytes 193544 | tf_op jit(solution)/shard_map/ppermute | solution.py:15
  3.3 4.5 %collective-permute-start.1 = (bf16[7,2,2,1152]{3,2,1,0:T(2,128)(2,1)S(1)}, bf16[7,2,2,1152]{3,2,1,0:T(2,128)(2,1)S(1)}, u32[]{:S(2)}, u32[]{:S(2)}) collective-permute-start(bf16[7,2,2,1152]{3,2,1,0:T(2,128)(2,1)S(1)} %get-tuple-element.10), channel_id=1, source_target_pairs={{64,0},{128,64},{192,128},{256,192},{320,256},{384,320},{448,384},... | collective-permute-start | bytes 193544 | tf_op jit(solution)/shard_map/ppermute | solution.py:18
  7.8 0.7 broadcast_compare_fusion
  8.5 0.0 collective-permute-done
  8.5 1.2 collective-permute-done.1
  9.7 1.2 %pad_maximum_fusion = bf16[7,2,12,1152]{3,2,1,0:T(8,128)(2,1)S(1)} fusion(bf16[7,2,2,1152]{3,2,1,0:T(2,128)(2,1)S(1)} %collective-permute-done.1, bf16[1,2,8,1152]{3,2,1,0:T(8,128)(2,1)} %bitcast.97, bf16[6,2,8,1152]{3,2,1,0:T(8,128)(2,1)} %param.6, bf16[7,2,2,1152]{3,2,1,0:T(2,128)(2,1)S(1)} %collective-permute-done), kind=kLoop, calls=%fused_computation.24 | loop fusion | flops 1548288 | bytes 774144 | tf_op jit(solution)/shard_map/concatenate | solution.py:19
  10.9 0.1 slice_convert_fusion
  11.0 0.0 copy-done.2
  11.0 0.0 copy-done.1
  11.1 0.1 fusion.26
  11.1 0.3 fusion.21
  11.5 0.0 copy-done
  11.5 0.7 fusion.8
  12.2 0.0 copy-start.5
  12.2 0.0 copy-start.4
  12.2 0.5 reshape_reshape.3
  12.7 0.4 copy.35
  13.1 1.0 copy.36
  14.2 18.9 %all-to-all-start = ((bf16[16,4,6,2,144]{4,3,1,2,0:T(2,128)(2,1)}), bf16[16,4,6,2,144]{4,3,1,2,0:T(2,128)(2,1)S(1)}, u32[]{:S(2)}, u32[]{:S(2)}) async-start(bf16[16,4,6,2,144]{4,3,1,2,0:T(2,128)(2,1)} %copy.36), calls=%async_computation | async-start | bytes 786432 | tf_op jit(solution)/shard_map/all_to_all | solution.py:38
  33.1 0.0 copy-done.5
  33.1 0.0 copy-done.4
  33.1 0.3 convolution_bitcast_fusion.4
  33.4 24.3 %all-to-all-done = bf16[16,4,6,2,144]{4,3,1,2,0:T(2,128)(2,1)S(1)} async-done(((bf16[16,4,6,2,144]{4,3,1,2,0:T(2,128)(2,1)}), bf16[16,4,6,2,144]{4,3,1,2,0:T(2,128)(2,1)S(1)}, u32[]{:S(2)}, u32[]{:S(2)}) %all-to-all-start) | async-done | bytes 221216 | tf_op jit(solution)/shard_map/all_to_all | solution.py:38
  57.7 1.2 copy.37
  58.9 6.4 %all-to-all-start.1 = ((bf16[16,4,6,2,144]{4,3,0,2,1:T(2,128)(2,1)}), bf16[16,4,6,2,144]{4,3,0,2,1:T(2,128)(2,1)S(1)}, u32[]{:S(2)}, u32[]{:S(2)}) async-start(bf16[16,4,6,2,144]{4,3,0,2,1:T(2,128)(2,1)} %copy.37), calls=%async_computation.1 | async-start | bytes 786432 | tf_op jit(solution)/shard_map/all_to_all | solution.py:38
  65.2 0.8 iota_compare_fusion
  66.0 0.7 slice_bitcast_fusion.3
  66.7 8.9 %all-to-all-done.1 = bf16[16,4,6,2,144]{4,3,0,2,1:T(2,128)(2,1)S(1)} async-done(((bf16[16,4,6,2,144]{4,3,0,2,1:T(2,128)(2,1)}), bf16[16,4,6,2,144]{4,3,0,2,1:T(2,128)(2,1)S(1)}, u32[]{:S(2)}, u32[]{:S(2)}) %all-to-all-start.1) | async-done | bytes 221216 | tf_op jit(solution)/shard_map/all_to_all | solution.py:38
  75.6 0.3 copy.38
  75.9 0.3 copy.39
  76.2 0.4 reshape.66
  76.5 0.0 copy-start.3
  76.6 1.2 %fusion.15 = f32[6,128,144]{1,2,0:T(8,128)S(1)} fusion(bf16[6,128,144]{2,1,0:T(8,128)(2,1)S(1)} %reshape.66, f32[128,144]{0,1:T(8,128)} %get-tuple-element.8, pred[4,128,128]{2,1,0:T(32,128)(4,1)} %iota_compare_fusion), kind=kOutput, calls=%fused_computation.13 | convolution fusion | flops 28422144 | bytes 753664 | tf_op jit(solution)/shard_map/ts,fsp->ftp/dot_general | solution.py:98
  77.8 1.2 fusion.16
  79.0 1.0 fusion.17
  79.9 0.0 copy-done.3
  79.9 1.0 fusion.18
  80.9 0.4 copy.44
  81.3 0.6 reshape.75
  81.9 34.7 %all_to_all.25 = bf16[64,2,864]{2,1,0:T(2,128)(2,1)} all-to-all(bf16[64,2,864]{2,1,0:T(2,128)(2,1)S(1)} %reshape.75), channel_id=1, replica_groups=mesh['lat'=16,'lev_0'=16,'lev_1'=4] {'lev_0','lev_1'}, dimensions={0} | all-to-all | bytes 442368 | tf_op jit(solution)/shard_map/all_to_all | solution.py:102
  116.6 1.5 %reshape.76 = bf16[128,6,144]{2,1,0:T(8,128)(2,1)S(1)} reshape(bf16[64,2,864]{2,1,0:T(2,128)(2,1)} %all_to_all.25) | data formatting | bytes 442368
  118.1 0.3 copy.56
  118.4 0.1 copy.46
  118.5 1.0 reshape.67
  (4 shorter events, 0.1 us)
Async XLA Ops:
  0.0 11.5 %copy-start = (bf16[1152,1152]{1,0:T(8,128)(2,1)S(1)}, bf16[1152,1152]{1,0:T(8,128)(2,1)}, u32[]{:S(2)}) copy-start(bf16[1152,1152]{1,0:T(8,128)(2,1)} %param.8) | copy-start | bytes 7962628
  0.0 11.0 %copy-start.2 = (bf16[2,8,1152]{2,1,0:T(8,128)(2,1)S(1)}, bf16[2,8,1152]{2,1,0:T(8,128)(2,1)}, u32[]{:S(2)}) copy-start(bf16[2,8,1152]{2,1,0:T(8,128)(2,1)} %param.7) | copy-start | bytes 110596
  0.0 11.0 %copy-start.1 = (bf16[6,2,8,1152]{3,2,1,0:T(8,128)(2,1)S(1)}, bf16[6,2,8,1152]{3,2,1,0:T(8,128)(2,1)}, u32[]{:S(2)}) copy-start(bf16[6,2,8,1152]{3,2,1,0:T(8,128)(2,1)} %param.6) | copy-start | bytes 663556
  1.3 7.2 %collective-permute-start = (bf16[7,2,2,1152]{3,2,1,0:T(2,128)(2,1)S(1)}, bf16[7,2,2,1152]{3,2,1,0:T(2,128)(2,1)S(1)}, u32[]{:S(2)}, u32[]{:S(2)}) collective-permute-start(bf16[7,2,2,1152]{3,2,1,0:T(2,128)(2,1)S(1)} %get-tuple-element.9), channel_id=1, source_target_pairs={{0,64},{64,128},{128,192},{192,256},{256,320},{320,384},{384,448},... | collective-permute-start | bytes 193544 | tf_op jit(solution)/shard_map/ppermute | solution.py:15
  3.3 6.4 %collective-permute-start.1 = (bf16[7,2,2,1152]{3,2,1,0:T(2,128)(2,1)S(1)}, bf16[7,2,2,1152]{3,2,1,0:T(2,128)(2,1)S(1)}, u32[]{:S(2)}, u32[]{:S(2)}) collective-permute-start(bf16[7,2,2,1152]{3,2,1,0:T(2,128)(2,1)S(1)} %get-tuple-element.10), channel_id=1, source_target_pairs={{64,0},{128,64},{192,128},{256,192},{320,256},{384,320},{448,384},... | collective-permute-start | bytes 193544 | tf_op jit(solution)/shard_map/ppermute | solution.py:18
  12.2 20.9 %copy-start.5 = (s32[128]{0:T(128)S(1)}, s32[128]{0:T(128)}, u32[]{:S(2)}) copy-start(s32[128]{0:T(128)} %param.10) | copy-start | bytes 1540
  12.2 20.9 %copy-start.4 = (f32[8,128,4]{1,2,0:T(4,128)S(1)}, f32[8,128,4]{1,2,0:T(4,128)}, u32[]{:S(2)}) copy-start(f32[8,128,4]{1,2,0:T(4,128)} %param.11) | copy-start | bytes 49156
  14.2 43.5 %all-to-all-start = ((bf16[16,4,6,2,144]{4,3,1,2,0:T(2,128)(2,1)}), bf16[16,4,6,2,144]{4,3,1,2,0:T(2,128)(2,1)S(1)}, u32[]{:S(2)}, u32[]{:S(2)}) async-start(bf16[16,4,6,2,144]{4,3,1,2,0:T(2,128)(2,1)} %copy.36), calls=%async_computation | async-start | bytes 786432 | tf_op jit(solution)/shard_map/all_to_all | solution.py:38
  58.9 16.8 %all-to-all-start.1 = ((bf16[16,4,6,2,144]{4,3,0,2,1:T(2,128)(2,1)}), bf16[16,4,6,2,144]{4,3,0,2,1:T(2,128)(2,1)S(1)}, u32[]{:S(2)}, u32[]{:S(2)}) async-start(bf16[16,4,6,2,144]{4,3,0,2,1:T(2,128)(2,1)} %copy.37), calls=%async_computation.1 | async-start | bytes 786432 | tf_op jit(solution)/shard_map/all_to_all | solution.py:38
  76.5 3.4 %copy-start.3 = (f32[128,144]{0,1:T(8,128)S(1)}, f32[128,144]{0,1:T(8,128)}, u32[]{:S(2)}) copy-start(f32[128,144]{0,1:T(8,128)} %get-tuple-element.5) | copy-start | bytes 221188
where the time goes:
time: 120 us
  blocking collectives  34.7 us (29%)
  waiting for transfers between devices  34.4 us (29%)
  starting transfers between devices  31.7 us (26%)
  local copies, waits for them, and re-layouts  8.58 us (7%)
  matrix products  5.33 us (4%)
  other arithmetic  4.52 us (4%)
    all_to_all x1, blocking collectives, on_device(): lax.all_to_all(total.astype(jnp.bfloat16), LEV, split_axis=1, concat_axis...  34.7 us
    all_to_all x2, waiting for transfers between devices, exchange_in_order(): lax.all_to_all(pieces, axes[k], split_axis=k, concat_axis=k, tiled=True)  33.2 us
    all_to_all x2, starting transfers between devices, exchange_in_order(): lax.all_to_all(pieces, axes[k], split_axis=k, concat_axis=k, tiled=True)  25.2 us
    ppermute x1, starting transfers between devices, padded_2(): lax.ppermute(lax.slice_in_dim(block, 0, width, axis=dim), axis, backward)  4.54 us
    dot_general x4, matrix products, on_device(): jnp.einsum('ts,fsp->ftp', selection[offset], columns, preferred_element_t...  4.33 us
  transfers between devices with their start and end apart: 4, of which 3 were waited for; matrix products, arithmetic and copies ran while one was open for 2% of the time, Pallas kernels for 0%

commit v1 on v0

v1 whole, which is shorter than its diff:
```python
import functools

import jax
import jax.numpy as jnp
from jax import lax
from jax.experimental import pallas as pl
from jax.experimental.pallas import tpu as pltpu
from jax.sharding import PartitionSpec as P

LANES = 128
MESH = pl.DeviceIdType.MESH


def kernel(
    fields_hbm, courant_hbm, matrix_hbm, mask_ref, start_ref, weight_ref, out_ref,
    fields_ref, courant_ref, matrix_ref, field_low, field_high, courant_low, courant_high,
    extended, speed, moved, moved_low, filtered, columns, spread, remapped,
    load_sem, halo_send, halo_recv, column_send, column_recv, back_send, back_recv,
    *, lat_count, lev_count,
):
    field_count, level_rows, lat_rows, lon_total = fields_hbm.shape
    planes = field_count * level_rows
    tiles = lon_total // LANES
    units = field_count * tiles
    level_total = level_rows * lev_count
    band_width = weight_ref.shape[1]
    lat = lax.axis_index("lat")
    lev = lax.axis_index("lev")

    def owner_of(q):
        return lax.div((q + 1) * lev_count + units - 1, units) - 1

    unit = lax.div(lev * units, lev_count)
    active = lax.div((lev + 1) * units, lev_count) > unit
    unit_field = lax.div(unit, tiles)
    unit_lanes = pl.ds(pl.multiple_of(lax.rem(unit, tiles) * LANES, LANES), LANES)
    polar = (lat < lat_count // 4) | (lat >= lat_count - lat_count // 4)
    has_low = lat > 0
    has_high = lat < lat_count - 1

    loads = [
        pltpu.make_async_copy(fields_hbm, fields_ref, load_sem.at[0]),
        pltpu.make_async_copy(courant_hbm, courant_ref, load_sem.at[1]),
    ]
    for load in loads:
        load.start()
    load_matrix = pltpu.make_async_copy(matrix_hbm, matrix_ref, load_sem.at[2])
    load_matrix.start()

    barrier = pltpu.get_barrier_semaphore()

    @pl.when(has_low)
    def _():
        pl.semaphore_signal(barrier, inc=1, device_id={"lat": lat - 1}, device_id_type=MESH)

    @pl.when(has_high)
    def _():
        pl.semaphore_signal(barrier, inc=1, device_id={"lat": lat + 1}, device_id_type=MESH)

    def greet(i, carry):
        peer = lax.rem(lev + i, lev_count)
        pl.semaphore_signal(barrier, inc=1, device_id={"lev": peer}, device_id_type=MESH)
        return carry

    lax.fori_loop(1, lev_count, greet, 0)

    @pl.when(active)
    def _():
        group = 8

        def spread_group(g, weights):
            rolled = []
            for b in range(band_width):
                for k in range(group):
                    spread[g * group + k, b] = jnp.broadcast_to(
                        weights[b][:, k : k + 1], (lat_rows, LANES)
                    )
                rolled.append(pltpu.roll(weights[b], LANES - group, 1))
            return tuple(rolled)

        lax.fori_loop(
            0,
            level_total // group,
            spread_group,
            tuple(weight_ref[:, b, :] for b in range(band_width)),
        )

    for load in loads:
        load.wait()

    pl.semaphore_wait(
        barrier, lev_count - 1 + jnp.where(has_low, 1, 0) + jnp.where(has_high, 1, 0)
    )

    def halo_copies(up):
        rows = pl.ds(lat_rows - 2, 2) if up else pl.ds(0, 2)
        to = lat + 1 if up else lat - 1
        side = 0 if up else 1
        pairs = (
            (fields_ref, field_low if up else field_high),
            (courant_ref, courant_low if up else courant_high),
        )
        return [
            pltpu.make_async_remote_copy(
                src_ref=source.at[..., rows, :],
                dst_ref=target,
                send_sem=halo_send.at[side, k],
                recv_sem=halo_recv.at[side, k],
                device_id={"lat": to},
                device_id_type=MESH,
            )
            for k, (source, target) in enumerate(pairs)
        ]

    @pl.when(has_high)
    def _():
        for copy in halo_copies(True):
            copy.start()

    @pl.when(has_low)
    def _():
        for copy in halo_copies(False):
            copy.start()

    own = pl.ds(8, lat_rows)
    for f in range(field_count):
        for l in range(level_rows):
            extended[f * level_rows + l, own, :] = fields_ref[f, l].astype(jnp.float32)
    for l in range(level_rows):
        speed[l, own, :] = courant_ref[l].astype(jnp.float32)

    def fill(rows, field_halo, courant_halo, there, side):
        @pl.when(there)
        def _():
            for copy in halo_copies(side == 0):
                copy.wait_recv()
            for f in range(field_count):
                for l in range(level_rows):
                    extended[f * level_rows + l, rows, :] = field_halo[f, l].astype(jnp.float32)
            for l in range(level_rows):
                speed[l, rows, :] = courant_halo[l].astype(jnp.float32)

        @pl.when(jnp.logical_not(there))
        def _():
            for p in range(planes):
                extended[p, rows, :] = jnp.zeros((2, lon_total), jnp.float32)
            for l in range(level_rows):
                speed[l, rows, :] = jnp.zeros((2, lon_total), jnp.float32)

    fill(pl.ds(6, 2), field_low, courant_low, has_low, 0)
    fill(pl.ds(8 + lat_rows, 2), field_high, courant_high, has_high, 1)

    row = lax.broadcasted_iota(jnp.int32, (lat_rows, lon_total), 0)
    live_low = jnp.where((row > 0) | has_low, 0.5 / 12.0, 0.0)
    live_high = jnp.where((row < lat_rows - 1) | has_high, 0.5 / 12.0, 0.0)

    def at(ref, p, shift):
        return ref[p, pl.ds(8 + shift, lat_rows), :]

    for l in range(level_rows):
        centre = at(speed, l, 0)
        low = (at(speed, l, -1) + centre) * live_low
        high = (centre + at(speed, l, 1)) * live_high
        for f in range(field_count):
            p = f * level_rows + l
            q = [at(extended, p, shift) for shift in (-2, -1, 0, 1, 2)]
            flux_low = low * (7.0 * (q[1] + q[2]) - (q[0] + q[3]))
            flux_high = high * (7.0 * (q[2] + q[3]) - (q[1] + q[4]))
            result = q[2] - (flux_high - flux_low)
            moved[p] = result

    load_matrix.wait()

    @pl.when(polar)
    def _():
        for f in range(field_count):
            both = moved[pl.ds(f * level_rows, level_rows)]
            moved_low[pl.ds(f * level_rows * lat_rows, level_rows * lat_rows), :] = both.reshape(
                level_rows * lat_rows, lon_total
            ).astype(jnp.bfloat16)

    small_row = lax.broadcasted_iota(jnp.int32, (lat_rows, LANES), 0)
    mask = jnp.zeros((lat_rows, LANES), jnp.int32)
    for j in range(lat_rows):
        mask = jnp.where(small_row == j, mask_ref[j], mask)

    def column_copy(q, lanes, f):
        return pltpu.make_async_remote_copy(
            src_ref=filtered.at[f, :, :, lanes],
            dst_ref=columns.at[pl.ds(lev * level_rows, level_rows)],
            send_sem=column_send,
            recv_sem=column_recv,
            device_id={"lev": owner_of(q)},
            device_id_type=MESH,
        )

    for first in range(0, tiles, 2):
        count = min(2, tiles - first)
        width = count * LANES
        lanes = pl.ds(first * LANES, width)

        @pl.when(polar)
        def _():
            correction = jnp.dot(
                moved_low[...], matrix_ref[:, lanes], preferred_element_type=jnp.float32
            ).reshape(field_count, level_rows, lat_rows, width)
            wide_mask = jnp.concatenate([mask] * count, axis=1) == 1
            kept = jnp.where(wide_mask[None, None], correction, 0.0)
            total = moved[:, :, lanes].reshape(kept.shape) + kept
            filtered[:, :, :, lanes] = total.astype(jnp.bfloat16)

        @pl.when(jnp.logical_not(polar))
        def _():
            filtered[:, :, :, lanes] = (
                moved[:, :, lanes]
                .reshape(field_count, level_rows, lat_rows, width)
                .astype(jnp.bfloat16)
            )

        def send_field(i, carry):
            f = lax.rem(i + lev, field_count)
            for k in range(count):
                q = f * tiles + first + k
                there = pl.ds((first + k) * LANES, LANES)

                @pl.when(owner_of(q) != lev)
                def _():
                    column_copy(q, there, f).start()

            return carry

        lax.fori_loop(0, field_count, send_field, 0)

    def sized(count):
        return columns.at[pl.ds(0, count * level_rows)]

    @pl.when(active)
    def _():
        columns[pl.ds(lev * level_rows, level_rows)] = filtered[unit_field, :, :, unit_lanes]
        pltpu.make_async_copy(sized(lev_count - 1), sized(lev_count - 1), column_recv).wait()

        def target(t):
            begin = start_ref[t]
            total = jnp.zeros((lat_rows, LANES), jnp.float32)
            for b in range(band_width):
                total = total + spread[t, b] * columns[begin + b].astype(jnp.float32)
            return total.astype(jnp.bfloat16)

        def send_back(i, carry):
            peer = lax.rem(lev + i, lev_count)
            place = pl.ds(peer * level_rows, level_rows)
            for l in range(level_rows):
                remapped[peer * level_rows + l] = target(peer * level_rows + l)
            pltpu.make_async_remote_copy(
                src_ref=remapped.at[place],
                dst_ref=out_ref.at[unit_field, :, :, unit_lanes],
                send_sem=back_send,
                recv_sem=back_recv,
                device_id={"lev": peer},
                device_id_type=MESH,
            ).start()
            return carry

        lax.fori_loop(1, lev_count, send_back, 0)
        for l in range(level_rows):
            out_ref[unit_field, l, :, unit_lanes] = target(lev * level_rows + l)
        pltpu.make_async_copy(sized(lev_count - 1), sized(lev_count - 1), back_send).wait()
        pltpu.make_async_copy(sized(units - 1), sized(units - 1), column_send).wait()
        pltpu.make_async_copy(sized(units - 1), sized(units - 1), back_recv).wait()

    @pl.when(jnp.logical_not(active))
    def _():
        pltpu.make_async_copy(sized(units), sized(units), column_send).wait()
        pltpu.make_async_copy(sized(units), sized(units), back_recv).wait()

    @pl.when(has_high)
    def _():
        for copy in halo_copies(True):
            copy.wait_send()

    @pl.when(has_low)
    def _():
        for copy in halo_copies(False):
            copy.wait_send()


def on_device(lat_count, lev_count, fields, courant, matrix, mask, start, weights):
    field_count, level_rows, lat_rows, lon_total = fields.shape
    planes = field_count * level_rows
    level_total = level_rows * lev_count
    band_width = weights.shape[2]
    bf16, f32 = jnp.bfloat16, jnp.float32
    anywhere = pl.BlockSpec(memory_space=pl.ANY)
    smem = pl.BlockSpec(memory_space=pltpu.SMEM)
    vmem = pl.BlockSpec(memory_space=pltpu.VMEM)
    return pl.pallas_call(
        functools.partial(kernel, lat_count=lat_count, lev_count=lev_count),
        out_shape=jax.ShapeDtypeStruct(fields.shape, bf16),
        in_specs=[anywhere, anywhere, anywhere, smem, smem, vmem],
        out_specs=vmem,
        scratch_shapes=[
            pltpu.VMEM(fields.shape, bf16),
            pltpu.VMEM(courant.shape, bf16),
            pltpu.VMEM(matrix.shape, bf16),
            pltpu.VMEM((field_count, level_rows, 2, lon_total), bf16),
            pltpu.VMEM((field_count, level_rows, 2, lon_total), bf16),
            pltpu.VMEM((level_rows, 2, lon_total), bf16),
            pltpu.VMEM((level_rows, 2, lon_total), bf16),
            pltpu.VMEM((planes, lat_rows + 16, lon_total), f32),
            pltpu.VMEM((level_rows, lat_rows + 16, lon_total), f32),
            pltpu.VMEM((planes, lat_rows, lon_total), f32),
            pltpu.VMEM((planes * lat_rows, lon_total), bf16),
            pltpu.VMEM(fields.shape, bf16),
            pltpu.VMEM((level_total, lat_rows, LANES), bf16),
            pltpu.VMEM((level_total, band_width, lat_rows, LANES), f32),
            pltpu.VMEM((level_total, lat_rows, LANES), bf16),
            pltpu.SemaphoreType.DMA((3,)),
            pltpu.SemaphoreType.DMA((2, 2)),
            pltpu.SemaphoreType.DMA((2, 2)),
            pltpu.SemaphoreType.DMA,
            pltpu.SemaphoreType.DMA,
            pltpu.SemaphoreType.DMA,
            pltpu.SemaphoreType.DMA,
        ],
        compiler_params=pltpu.CompilerParams(
            collective_id=0, has_side_effects=True, vmem_limit_bytes=32 << 20
        ),
    )(fields, courant, matrix, mask, start, jnp.transpose(weights, (0, 2, 1)))


def solution(mesh):
    step = functools.partial(on_device, mesh.shape["lat"], mesh.shape["lev"])
    placed = (
        P(None, "lev", "lat", None),
        P("lev", "lat", None),
        P(),
        P("lat"),
        P(),
        P("lat", None, None),
    )
    return jax.shard_map(
        step, mesh=mesh, in_specs=placed, out_specs=P(None, "lev", "lat", None), check_vma=False
    )
```

time: 120 us -> 67 us (0.56)
  the two profiles are of different devices: /device:TPU:2 before, /device:TPU:6 now
where the time goes in v1:
time: 67 us; the launch traced here: 66.7 us
  Pallas kernels  60.5 us (90%)
  local copies, waits for them, and re-layouts  6.17 us (9%)
    pallas_call x1, Pallas kernels, on_device(): pl.pallas_call(functools.partial(kernel, lat_count=lat_count, lev_count=l...  60.5 us
    unnamed x13, local copies, waits for them, and re-layouts  6.17 us

profile of v1, /device:TPU:6, one launch (start us, length us, event | category | flops | bytes accessed | tf_op | source)
XLA Modules:
  0.0 66.7 jit_solution(4371670620959122160)
XLA Ops:
  0.0 0.0 copy-start
  0.0 1.7 %copy-done = bf16[1152,1152]{1,0:T(8,128)(2,1)S(1)} copy-done((bf16[1152,1152]{1,0:T(8,128)(2,1)S(1)}, bf16[1152,1152]{1,0:T(8,128)(2,1)}, u32[]{:S(2)}) %copy-start) | copy-done | bytes 2654232
  1.8 0.0 copy-start.1
  1.8 0.9 %copy-done.1 = bf16[6,2,8,1152]{3,2,1,0:T(8,128)(2,1)S(1)} copy-done((bf16[6,2,8,1152]{3,2,1,0:T(8,128)(2,1)S(1)}, bf16[6,2,8,1152]{3,2,1,0:T(8,128)(2,1)}, u32[]{:S(2)}) %copy-start.1) | copy-done | bytes 221208
  2.7 0.0 copy-start.2
  2.7 0.8 %copy-done.2 = bf16[2,8,1152]{2,1,0:T(8,128)(2,1)S(1)} copy-done((bf16[2,8,1152]{2,1,0:T(8,128)(2,1)S(1)}, bf16[2,8,1152]{2,1,0:T(8,128)(2,1)}, u32[]{:S(2)}) %copy-start.2) | copy-done | bytes 36888
  3.5 0.0 copy-start.3
  3.5 0.7 %copy-done.3 = f32[8,128,4]{1,2,0:T(4,128)S(1)} copy-done((f32[8,128,4]{1,2,0:T(4,128)S(1)}, f32[8,128,4]{1,2,0:T(4,128)}, u32[]{:S(2)}) %copy-start.3) | copy-done | bytes 16408
  4.2 0.0 copy-start.4
  4.2 0.7 copy-done.4
  4.8 0.0 copy-start.5
  4.8 0.7 copy-done.5
  5.5 60.5 %shard_map.64 = bf16[6,2,8,1152]{3,2,1,0:T(8,128)(2,1)S(1)} custom-call(bf16[6,2,8,1152]{3,2,1,0:T(8,128)(2,1)S(1)} %copy-done.1, bf16[2,8,1152]{2,1,0:T(8,128)(2,1)S(1)} %copy-done.2, bf16[1152,1152]{1,0:T(8,128)(2,1)S(1)} %copy-done, s32[8]{0:T(128)S(1)} %copy-done.4, s32[128]{0:T(128)S(1)} %copy-done.5, f32[8,4,128]{2,1,0:T(4,128)S(1)} %bitcast.1), custom_call_target="tpu_custom_call" | custom-call | tf_op jit(solution)/shard_map/pallas_call | solution.py:296
  66.0 0.7 %copy.8 = bf16[6,2,8,1152]{3,2,1,0:T(8,128)(2,1)} copy(bf16[6,2,8,1152]{3,2,1,0:T(8,128)(2,1)S(1)} %shard_map.64) | data formatting | bytes 442368
Async XLA Ops:
  0.0 1.7 %copy-start = (bf16[1152,1152]{1,0:T(8,128)(2,1)S(1)}, bf16[1152,1152]{1,0:T(8,128)(2,1)}, u32[]{:S(2)}) copy-start(bf16[1152,1152]{1,0:T(8,128)(2,1)} %matrix_hbm.1) | copy-start | bytes 7962628
  1.8 0.9 %copy-start.1 = (bf16[6,2,8,1152]{3,2,1,0:T(8,128)(2,1)S(1)}, bf16[6,2,8,1152]{3,2,1,0:T(8,128)(2,1)}, u32[]{:S(2)}) copy-start(bf16[6,2,8,1152]{3,2,1,0:T(8,128)(2,1)} %fields_hbm.1) | copy-start | bytes 663556
  2.7 0.8 %copy-start.2 = (bf16[2,8,1152]{2,1,0:T(8,128)(2,1)S(1)}, bf16[2,8,1152]{2,1,0:T(8,128)(2,1)}, u32[]{:S(2)}) copy-start(bf16[2,8,1152]{2,1,0:T(8,128)(2,1)} %courant_hbm.1) | copy-start | bytes 110596
  3.5 0.7 %copy-start.3 = (f32[8,128,4]{1,2,0:T(4,128)S(1)}, f32[8,128,4]{1,2,0:T(4,128)}, u32[]{:S(2)}) copy-start(f32[8,128,4]{1,2,0:T(4,128)} %param.11) | copy-start | bytes 49156
  4.2 0.7 copy-start.4
  4.8 0.7 copy-start.5

commit v2 on v1

--- a/solution.py
+++ b/solution.py
@@ -15,8 +15,8 @@
     fields_hbm, courant_hbm, matrix_hbm, mask_ref, start_ref, weight_ref, out_ref,
     fields_ref, courant_ref, matrix_ref, field_low, field_high, courant_low, courant_high,
     extended, speed, moved, moved_low, filtered, columns, spread, remapped,
-    load_sem, halo_send, halo_recv, column_send, column_recv, back_send, back_recv,
-    *, lat_count, lev_count,
+    load_sem, ready, halo_send, halo_recv, column_send, column_recv, back_send, back_recv,
+    *, lat_count, lev_count, group_size,
 ):
     field_count, level_rows, lat_rows, lon_total = fields_hbm.shape
     planes = field_count * level_rows
@@ -27,11 +27,20 @@
     lat = lax.axis_index("lat")
     lev = lax.axis_index("lev")
 
-    def owner_of(q):
-        return lax.div((q + 1) * lev_count + units - 1, units) - 1
-
-    unit = lax.div(lev * units, lev_count)
-    active = lax.div((lev + 1) * units, lev_count) > unit
+    spare = lev_count - units
+    first_spare = units // 2
+
+    def owns(d):
+        return (d < first_spare) | (d >= first_spare + spare)
+
+    def unit_of(d):
+        return jnp.where(d < first_spare, d, d - spare)
+
+    active = owns(lev)
+    unit = jnp.where(active, unit_of(lev), 0)
+    group = lax.div(lev, group_size)
+    groups = lev_count // group_size
+    ready_count = (group + 1) * group_size
     unit_field = lax.div(unit, tiles)
     unit_lanes = pl.ds(pl.multiple_of(lax.rem(unit, tiles) * LANES, LANES), LANES)
     polar = (lat < lat_count // 4) | (lat >= lat_count - lat_count // 4)
@@ -57,39 +66,20 @@
     def _():
         pl.semaphore_signal(barrier, inc=1, device_id={"lat": lat + 1}, device_id_type=MESH)
 
-    def greet(i, carry):
-        peer = lax.rem(lev + i, lev_count)
-        pl.semaphore_signal(barrier, inc=1, device_id={"lev": peer}, device_id_type=MESH)
+    def greet(peer, carry):
+        @pl.when(peer != lev)
+        def _():
+            pl.semaphore_signal(barrier, inc=1, device_id={"lev": peer}, device_id_type=MESH)
+
         return carry
 
-    lax.fori_loop(1, lev_count, greet, 0)
-
-    @pl.when(active)
-    def _():
-        group = 8
-
-        def spread_group(g, weights):
-            rolled = []
-            for b in range(band_width):
-                for k in range(group):
-                    spread[g * group + k, b] = jnp.broadcast_to(
-                        weights[b][:, k : k + 1], (lat_rows, LANES)
-                    )
-                rolled.append(pltpu.roll(weights[b], LANES - group, 1))
-            return tuple(rolled)
-
-        lax.fori_loop(
-            0,
-            level_total // group,
-            spread_group,
-            tuple(weight_ref[:, b, :] for b in range(band_width)),
-        )
+    lax.fori_loop(group * group_size, lev_count, greet, 0)
 
     for load in loads:
         load.wait()
 
     pl.semaphore_wait(
-        barrier, lev_count - 1 + jnp.where(has_low, 1, 0) + jnp.where(has_high, 1, 0)
+        barrier, ready_count - 1 + jnp.where(has_low, 1, 0) + jnp.where(has_high, 1, 0)
     )
 
     def halo_copies(up):
@@ -122,6 +112,14 @@
         for copy in halo_copies(False):
             copy.start()
 
+    def announce(peer, carry):
+        pl.semaphore_signal(
+            ready.at[group], inc=1, device_id={"lev": peer}, device_id_type=MESH
+        )
+        return carry
+
+    lax.fori_loop(0, group * group_size, announce, 0)
+
     own = pl.ds(8, lat_rows)
     for f in range(field_count):
         for l in range(level_rows):
@@ -184,16 +182,6 @@
     for j in range(lat_rows):
         mask = jnp.where(small_row == j, mask_ref[j], mask)
 
-    def column_copy(q, lanes, f):
-        return pltpu.make_async_remote_copy(
-            src_ref=filtered.at[f, :, :, lanes],
-            dst_ref=columns.at[pl.ds(lev * level_rows, level_rows)],
-            send_sem=column_send,
-            recv_sem=column_recv,
-            device_id={"lev": owner_of(q)},
-            device_id_type=MESH,
-        )
-
     for first in range(0, tiles, 2):
         count = min(2, tiles - first)
         width = count * LANES
@@ -217,19 +205,59 @@
                 .astype(jnp.bfloat16)
             )
 
-        def send_field(i, carry):
-            f = lax.rem(i + lev, field_count)
-            for k in range(count):
-                q = f * tiles + first + k
-                there = pl.ds((first + k) * LANES, LANES)
-
-                @pl.when(owner_of(q) != lev)
-                def _():
-                    column_copy(q, there, f).start()
-
+    def send_to(d):
+        @pl.when(owns(d) & (d != lev))
+        def _():
+            q = unit_of(d)
+            lanes = pl.ds(pl.multiple_of(lax.rem(q, tiles) * LANES, LANES), LANES)
+            pltpu.make_async_remote_copy(
+                src_ref=filtered.at[lax.div(q, tiles), :, :, lanes],
+                dst_ref=columns.at[pl.ds(lev * level_rows, level_rows)],
+                send_sem=column_send,
+                recv_sem=column_recv,
+                device_id={"lev": d},
+                device_id_type=MESH,
+            ).start()
+
+    def send_ready(i, carry):
+        step = lax.div(i + 1, 2)
+        step = jnp.where(lax.rem(i, 2) == 1, step, ready_count - step)
+        send_to(lax.rem(lev + lev_count // 2 + step, ready_count))
+        return carry
+
+    lax.fori_loop(0, ready_count, send_ready, 0)
+
+    def send_later(h, carry):
+        pl.semaphore_wait(ready.at[h], group_size)
+
+        def each(k, carry):
+            send_to(h * group_size + k)
             return carry
 
-        lax.fori_loop(0, field_count, send_field, 0)
+        return lax.fori_loop(0, group_size, each, carry)
+
+    lax.fori_loop(group + 1, groups, send_later, 0)
+
+    @pl.when(active)
+    def _():
+        group = 8
+
+        def spread_group(g, weights):
+            rolled = []
+            for b in range(band_width):
+                for k in range(group):
+                    spread[g * group + k, b] = jnp.broadcast_to(
+                        weights[b][:, k : k + 1], (lat_rows, LANES)
+                    )
+                rolled.append(pltpu.roll(weights[b], LANES - group, 1))
+            return tuple(rolled)
+
+        lax.fori_loop(
+            0,
+            level_total // group,
+            spread_group,
+            tuple(weight_ref[:, b, :] for b in range(band_width)),
+        )
 
     def sized(count):
         return columns.at[pl.ds(0, count * level_rows)]
@@ -247,7 +275,7 @@
             return total.astype(jnp.bfloat16)
 
         def send_back(i, carry):
-            peer = lax.rem(lev + i, lev_count)
+            peer = jnp.where(i <= lev, i - 1, i)
             place = pl.ds(peer * level_rows, level_rows)
             for l in range(level_rows):
                 remapped[peer * level_rows + l] = target(peer * level_rows + l)
@@ -287,6 +315,7 @@
 def on_device(lat_count, lev_count, fields, courant, matrix, mask, start, weights):
     field_count, level_rows, lat_rows, lon_total = fields.shape
     planes = field_count * level_rows
+    group_size = 4
     level_total = level_rows * lev_count
     band_width = weights.shape[2]
     bf16, f32 = jnp.bfloat16, jnp.float32
@@ -294,7 +323,9 @@
     smem = pl.BlockSpec(memory_space=pltpu.SMEM)
     vmem = pl.BlockSpec(memory_space=pltpu.VMEM)
     return pl.pallas_call(
-        functools.partial(kernel, lat_count=lat_count, lev_count=lev_count),
+        functools.partial(
+            kernel, lat_count=lat_count, lev_count=lev_count, group_size=group_size
+        ),
         out_shape=jax.ShapeDtypeStruct(fields.shape, bf16),
         in_specs=[anywhere, anywhere, anywhere, smem, smem, vmem],
         out_specs=vmem,
@@ -315,6 +346,7 @@
             pltpu.VMEM((level_total, band_width, lat_rows, LANES), f32),
             pltpu.VMEM((level_total, lat_rows, LANES), bf16),
             pltpu.SemaphoreType.DMA((3,)),
+            pltpu.SemaphoreType.REGULAR((lev_count // group_size,)),
             pltpu.SemaphoreType.DMA((2, 2)),
             pltpu.SemaphoreType.DMA((2, 2)),
             pltpu.SemaphoreType.DMA,
@@ -323,7 +355,7 @@
             pltpu.SemaphoreType.DMA,
         ],
         compiler_params=pltpu.CompilerParams(
-            collective_id=0, has_side_effects=True, vmem_limit_bytes=32 << 20
+            collective_id=0, has_side_effects=True, vmem_limit_bytes=63 << 20
         ),
     )(fields, courant, matrix, mask, start, jnp.transpose(weights, (0, 2, 1)))
 

time: 67 us -> 56.2 us (0.84)
  Pallas kernels: 60.5 us -> 53.8 us
  local copies, waits for them, and re-layouts: 6.17 us -> 1.64 us
    pallas_call x1, Pallas kernels: 60.5 us -> 53.8 us  [on_device(): pl.pallas_call(functools.partial(kernel, lat_count=lat_count, lev_count=l...]
    unnamed x13 -> x1, local copies, waits for them, and re-layouts: 6.17 us -> 1.64 us
where the time goes in v2:
time: 56.2 us; the launch traced here: 55.5 us
  Pallas kernels  53.8 us (96%)
  local copies, waits for them, and re-layouts  1.64 us (3%)
    pallas_call x1, Pallas kernels, on_device(): pl.pallas_call(functools.partial(kernel, lat_count=lat_count, lev_count=l...  53.8 us
    unnamed x1, local copies, waits for them, and re-layouts  1.64 us

profile of v2, /device:TPU:6, one launch (start us, length us, event | category | flops | bytes accessed | tf_op | source)
XLA Modules:
  0.0 55.5 jit_solution(9315018789106389801)
XLA Ops:
  0.0 53.8 %shard_map.64 = bf16[6,2,8,1152]{3,2,1,0:T(8,128)(2,1)} custom-call(bf16[6,2,8,1152]{3,2,1,0:T(8,128)(2,1)} %fields_hbm.1, bf16[2,8,1152]{2,1,0:T(8,128)(2,1)} %courant_hbm.1, bf16[1152,1152]{1,0:T(8,128)(2,1)} %matrix_hbm.1, s32[8]{0:T(128)} %mask_ref.1, s32[128]{0:T(128)} %start_ref.1, f32[8,4,128]{2,1,0:T(4,128)} %bitcast.1), custom_call_target="tpu_custom_call" | custom-call | tf_op jit(solution)/shard_map/pallas_call | solution.py:325
  53.8 1.6 %copy.8 = bf16[6,2,8,1152]{3,2,1,0:T(8,128)(2,1)} copy(bf16[6,2,8,1152]{3,2,1,0:T(8,128)(2,1)} %shard_map.64) | data formatting | bytes 442368

commit v3 on v2

--- a/solution.py
+++ b/solution.py
@@ -12,10 +12,10 @@
 
 
 def kernel(
-    fields_hbm, courant_hbm, matrix_hbm, mask_ref, start_ref, weight_ref, out_ref,
-    fields_ref, courant_ref, matrix_ref, field_low, field_high, courant_low, courant_high,
+    fields_hbm, courant_hbm, matrix_hbm, mask_hbm, start_hbm, weight_hbm, out_ref,
+    mask_ref, start_ref, weight_ref, fields_ref, courant_ref, matrix_ref, field_low, field_high, courant_low, courant_high,
     extended, speed, moved, moved_low, filtered, columns, spread, remapped,
-    load_sem, ready, halo_send, halo_recv, column_send, column_recv, back_send, back_recv,
+    load_sem, place_sem, ready, halo_send, halo_recv, column_send, column_recv, back_send, back_recv,
     *, lat_count, lev_count, group_size,
 ):
     field_count, level_rows, lat_rows, lon_total = fields_hbm.shape
@@ -28,13 +28,17 @@
     lev = lax.axis_index("lev")
 
     spare = lev_count - units
-    first_spare = units // 2
+    whole_groups = lev_count // group_size - spare
+    slot = group_size // 2
+    full = whole_groups * group_size
 
     def owns(d):
-        return (d < first_spare) | (d >= first_spare + spare)
+        return (d < full) | (lax.rem(d, group_size) != slot)
 
     def unit_of(d):
-        return jnp.where(d < first_spare, d, d - spare)
+        later = lax.div(d, group_size) - whole_groups
+        passed = later + jnp.where(lax.rem(d, group_size) > slot, 1, 0)
+        return d - jnp.where(d < full, 0, passed)
 
     active = owns(lev)
     unit = jnp.where(active, unit_of(lev), 0)
@@ -53,8 +57,19 @@
     ]
     for load in loads:
         load.start()
-    load_matrix = pltpu.make_async_copy(matrix_hbm, matrix_ref, load_sem.at[2])
-    load_matrix.start()
+    late_loads = [
+        pltpu.make_async_copy(source, target, load_sem.at[2 + k])
+        for k, (source, target) in enumerate(
+            (
+                (mask_hbm, mask_ref),
+                (matrix_hbm, matrix_ref),
+                (start_hbm, start_ref),
+                (weight_hbm, weight_ref),
+            )
+        )
+    ]
+    for load in late_loads:
+        load.start()
 
     barrier = pltpu.get_barrier_semaphore()
 
@@ -167,7 +182,8 @@
             result = q[2] - (flux_high - flux_low)
             moved[p] = result
 
-    load_matrix.wait()
+    for load in late_loads:
+        load.wait()
 
     @pl.when(polar)
     def _():
@@ -182,33 +198,16 @@
     for j in range(lat_rows):
         mask = jnp.where(small_row == j, mask_ref[j], mask)
 
-    for first in range(0, tiles, 2):
-        count = min(2, tiles - first)
-        width = count * LANES
-        lanes = pl.ds(first * LANES, width)
-
-        @pl.when(polar)
-        def _():
-            correction = jnp.dot(
-                moved_low[...], matrix_ref[:, lanes], preferred_element_type=jnp.float32
-            ).reshape(field_count, level_rows, lat_rows, width)
-            wide_mask = jnp.concatenate([mask] * count, axis=1) == 1
-            kept = jnp.where(wide_mask[None, None], correction, 0.0)
-            total = moved[:, :, lanes].reshape(kept.shape) + kept
-            filtered[:, :, :, lanes] = total.astype(jnp.bfloat16)
-
-        @pl.when(jnp.logical_not(polar))
-        def _():
-            filtered[:, :, :, lanes] = (
-                moved[:, :, lanes]
-                .reshape(field_count, level_rows, lat_rows, width)
-                .astype(jnp.bfloat16)
-            )
-
-    def send_to(d):
-        @pl.when(owns(d) & (d != lev))
-        def _():
-            q = unit_of(d)
+    def owner_of(q):
+        rest = jnp.maximum(q - full, 0)
+        place = lax.rem(rest, group_size - 1)
+        place = place + jnp.where(place >= slot, 1, 0)
+        later = full + lax.div(rest, group_size - 1) * group_size + place
+        return jnp.where(q < full, q, later)
+
+    def send(q, d):
+        @pl.when(d != lev)
+        def _():
             lanes = pl.ds(pl.multiple_of(lax.rem(q, tiles) * LANES, LANES), LANES)
             pltpu.make_async_remote_copy(
                 src_ref=filtered.at[lax.div(q, tiles), :, :, lanes],
@@ -219,13 +218,50 @@
                 device_id_type=MESH,
             ).start()
 
-    def send_ready(i, carry):
-        step = lax.div(i + 1, 2)
-        step = jnp.where(lax.rem(i, 2) == 1, step, ready_count - step)
-        send_to(lax.rem(lev + lev_count // 2 + step, ready_count))
-        return carry
-
-    lax.fori_loop(0, ready_count, send_ready, 0)
+    def send_to(d):
+        @pl.when(owns(d))
+        def _():
+            send(unit_of(d), d)
+
+    far_field = lax.div(
+        lev * field_count, lev_count
+    )
+
+    for first in range(0, tiles, 2):
+        count = min(2, tiles - first)
+        width = count * LANES
+        lanes = pl.ds(first * LANES, width)
+
+        @pl.when(polar)
+        def _():
+            correction = jnp.dot(
+                moved_low[...], matrix_ref[:, lanes], preferred_element_type=jnp.float32
+            ).reshape(field_count, level_rows, lat_rows, width)
+            wide_mask = jnp.concatenate([mask] * count, axis=1) == 1
+            kept = jnp.where(wide_mask[None, None], correction, 0.0)
+            total = moved[:, :, lanes].reshape(kept.shape) + kept
+            filtered[:, :, :, lanes] = total.astype(jnp.bfloat16)
+
+        @pl.when(jnp.logical_not(polar))
+        def _():
+            filtered[:, :, :, lanes] = (
+                moved[:, :, lanes]
+                .reshape(field_count, level_rows, lat_rows, width)
+                .astype(jnp.bfloat16)
+            )
+
+        def send_block(i, carry):
+            f = lax.rem(far_field + i, field_count)
+            for k in range(count):
+                q = f * tiles + first + k
+
+                @pl.when(owner_of(q) < ready_count)
+                def _():
+                    send(q, owner_of(q))
+
+            return carry
+
+        lax.fori_loop(0, field_count, send_block, 0)
 
     def send_later(h, carry):
         pl.semaphore_wait(ready.at[h], group_size)
@@ -291,10 +327,17 @@
 
         lax.fori_loop(1, lev_count, send_back, 0)
         for l in range(level_rows):
-            out_ref[unit_field, l, :, unit_lanes] = target(lev * level_rows + l)
+            remapped[lev * level_rows + l] = target(lev * level_rows + l)
+        keep = pltpu.make_async_copy(
+            remapped.at[pl.ds(lev * level_rows, level_rows)],
+            out_ref.at[unit_field, :, :, unit_lanes],
+            place_sem,
+        )
+        keep.start()
         pltpu.make_async_copy(sized(lev_count - 1), sized(lev_count - 1), back_send).wait()
         pltpu.make_async_copy(sized(units - 1), sized(units - 1), column_send).wait()
         pltpu.make_async_copy(sized(units - 1), sized(units - 1), back_recv).wait()
+        keep.wait()
 
     @pl.when(jnp.logical_not(active))
     def _():
@@ -320,16 +363,17 @@
     band_width = weights.shape[2]
     bf16, f32 = jnp.bfloat16, jnp.float32
     anywhere = pl.BlockSpec(memory_space=pl.ANY)
-    smem = pl.BlockSpec(memory_space=pltpu.SMEM)
-    vmem = pl.BlockSpec(memory_space=pltpu.VMEM)
     return pl.pallas_call(
         functools.partial(
             kernel, lat_count=lat_count, lev_count=lev_count, group_size=group_size
         ),
         out_shape=jax.ShapeDtypeStruct(fields.shape, bf16),
-        in_specs=[anywhere, anywhere, anywhere, smem, smem, vmem],
-        out_specs=vmem,
+        in_specs=[anywhere] * 6,
+        out_specs=anywhere,
         scratch_shapes=[
+            pltpu.SMEM(mask.shape, jnp.int32),
+            pltpu.SMEM(start.shape, jnp.int32),
+            pltpu.VMEM((weights.shape[0], band_width, level_total), f32),
             pltpu.VMEM(fields.shape, bf16),
             pltpu.VMEM(courant.shape, bf16),
             pltpu.VMEM(matrix.shape, bf16),
@@ -345,7 +389,8 @@
             pltpu.VMEM((level_total, lat_rows, LANES), bf16),
             pltpu.VMEM((level_total, band_width, lat_rows, LANES), f32),
             pltpu.VMEM((level_total, lat_rows, LANES), bf16),
-            pltpu.SemaphoreType.DMA((3,)),
+            pltpu.SemaphoreType.DMA((6,)),
+            pltpu.SemaphoreType.DMA,
             pltpu.SemaphoreType.REGULAR((lev_count // group_size,)),
             pltpu.SemaphoreType.DMA((2, 2)),
             pltpu.SemaphoreType.DMA((2, 2)),

time: 56.2 us -> 55.4 us (0.986)
  no operation moved by 1% of the time
where the time goes in v3:
time: 55.4 us; the launch traced here: 54.9 us
  Pallas kernels  53.3 us (96%)
  local copies, waits for them, and re-layouts  1.64 us (3%)
    pallas_call x1, Pallas kernels, on_device(): pl.pallas_call(functools.partial(kernel, lat_count=lat_count, lev_count=l...  53.3 us
    unnamed x1, local copies, waits for them, and re-layouts  1.64 us

profile of v3, /device:TPU:6, one launch (start us, length us, event | category | flops | bytes accessed | tf_op | source)
XLA Modules:
  0.0 54.9 jit_solution(2909113811625808436)
XLA Ops:
  0.0 53.3 %shard_map.64 = bf16[6,2,8,1152]{3,2,1,0:T(8,128)(2,1)} custom-call(bf16[6,2,8,1152]{3,2,1,0:T(8,128)(2,1)} %fields_hbm.1, bf16[2,8,1152]{2,1,0:T(8,128)(2,1)} %courant_hbm.1, bf16[1152,1152]{1,0:T(8,128)(2,1)} %matrix_hbm.1, s32[8]{0:T(128)} %mask_hbm.1, s32[128]{0:T(128)} %start_hbm.1, f32[8,4,128]{2,1,0:T(4,128)} %bitcast.1), custom_call_target="tpu_custom_call" | custom-call | tf_op jit(solution)/shard_map/pallas_call | solution.py:366
  53.3 1.6 %copy.8 = bf16[6,2,8,1152]{3,2,1,0:T(8,128)(2,1)} copy(bf16[6,2,8,1152]{3,2,1,0:T(8,128)(2,1)} %shard_map.64) | data formatting | bytes 442368

commit v4 on v3

--- a/solution.py
+++ b/solution.py
@@ -224,7 +224,7 @@
             send(unit_of(d), d)
 
     far_field = lax.div(
-        lev * field_count, lev_count
+        lax.rem(lev + lev_count // 2, lev_count) * field_count, lev_count
     )
 
     for first in range(0, tiles, 2):
@@ -310,8 +310,7 @@
                 total = total + spread[t, b] * columns[begin + b].astype(jnp.float32)
             return total.astype(jnp.bfloat16)
 
-        def send_back(i, carry):
-            peer = jnp.where(i <= lev, i - 1, i)
+        def send_piece(peer):
             place = pl.ds(peer * level_rows, level_rows)
             for l in range(level_rows):
                 remapped[peer * level_rows + l] = target(peer * level_rows + l)
@@ -323,9 +322,22 @@
                 device_id={"lev": peer},
                 device_id_type=MESH,
             ).start()
+
+        late = 3
+
+        def send_back(i, carry):
+            place = lax.rem(i, group_size)
+            plane = lax.div(i, group_size)
+            plane = plane - jnp.where(place == slot, late, jnp.where(place > slot, late - 1, 0))
+            peer = plane * group_size + place
+
+            @pl.when((plane >= 0) & (plane < groups) & (peer != lev))
+            def _():
+                send_piece(peer)
+
             return carry
 
-        lax.fori_loop(1, lev_count, send_back, 0)
+        lax.fori_loop(0, lev_count + late * group_size, send_back, 0)
         for l in range(level_rows):
             remapped[lev * level_rows + l] = target(lev * level_rows + l)
         keep = pltpu.make_async_copy(

time: 55.4 us -> 54.9 us (level)
  no operation moved by 1% of the time
where the time goes in v4:
time: 54.9 us; the launch traced here: 54.4 us
  Pallas kernels  52.8 us (96%)
  local copies, waits for them, and re-layouts  1.64 us (3%)
    pallas_call x1, Pallas kernels, on_device(): pl.pallas_call(functools.partial(kernel, lat_count=lat_count, lev_count=l...  52.8 us
    unnamed x1, local copies, waits for them, and re-layouts  1.64 us

profile of v4, /device:TPU:6, one launch (start us, length us, event | category | flops | bytes accessed | tf_op | source)
XLA Modules:
  0.0 54.4 jit_solution(7860739170723458772)
XLA Ops:
  0.0 52.8 %shard_map.64 = bf16[6,2,8,1152]{3,2,1,0:T(8,128)(2,1)} custom-call(bf16[6,2,8,1152]{3,2,1,0:T(8,128)(2,1)} %fields_hbm.1, bf16[2,8,1152]{2,1,0:T(8,128)(2,1)} %courant_hbm.1, bf16[1152,1152]{1,0:T(8,128)(2,1)} %matrix_hbm.1, s32[8]{0:T(128)} %mask_hbm.1, s32[128]{0:T(128)} %start_hbm.1, f32[8,4,128]{2,1,0:T(4,128)} %bitcast.1), custom_call_target="tpu_custom_call" | custom-call | tf_op jit(solution)/shard_map/pallas_call | solution.py:378
  52.8 1.6 %copy.8 = bf16[6,2,8,1152]{3,2,1,0:T(8,128)(2,1)} copy(bf16[6,2,8,1152]{3,2,1,0:T(8,128)(2,1)} %shard_map.64) | data formatting | bytes 442368
